TPU v7x, 256 devices: a whole 4x4x8 slice. The times are simulated.
256 devices in a mesh: seq: 64 (over z, x, core), head: 4 (over y).
Axes of the slice: x: 4, y: 4, z: 8, core: 2. Of those that a mesh axis runs over, the one named last changes fastest.
Arguments:
- qk: bfloat16 [65536, 2048], P('seq', 'head'), may hold values from -8 to 8
- values: bfloat16 [65536, 2048], P('seq', 'head'), may hold values from -6 to 6
- out_weight: bfloat16 [2048, 2048], P('head'), may hold values from -0.125 to 0.125
- out_cotangent: bfloat16 [65536, 2048], P('seq', 'head'), may hold values from -6 to 6
- cluster_ids: int32 [512, 16], P(None, 'head'), may hold values from 0 to 127, as said below
Outputs:
- output: bfloat16 [65536, 2048], P('seq', 'head')
- grad_qk: bfloat16 [65536, 2048], P('seq', 'head')
- grad_values: bfloat16 [65536, 2048], P('seq', 'head')
Inputs may be any that keep to these rules, and one draw needn't show every extreme that they name: `cluster_ids`: call c // 2 the owner of cluster c. Over the blocks of one seq index and the heads of one head index, at most 2 name clusters of one owner, and exactly 2 for some owner. For every head, the clusters of each owner hold exactly 8 blocks together, and some cluster holds all 8.
All inputs are finite; a program needn't handle non-finite values.
Results may differ from a plain program's by a relative error of at most 0.013.
Values may be sent and summed in bfloat16 or wider, within the bound.
A program may use at most 128 MiB of HBM per device.

v0:
```python
import jax
import jax.numpy as jnp
from jax import lax
from jax.sharding import PartitionSpec as P

BLOCK = 128
CL_OWN = 2
NEG_FILL = -1e30


def unit_forward(tokens_x, tokens_v, group):
    row_count = tokens_x.shape[0]
    block_rows = row_count // group.shape[0]
    inv_root = tokens_x.shape[1] ** (-0.5)
    scores = (
        jnp.einsum("rd,cd->rc", tokens_x, tokens_x, preferred_element_type=jnp.float32) * inv_root
    )
    row_group = jnp.repeat(group, block_rows)
    position = jnp.arange(row_count)
    allowed = (row_group[:, None] == row_group[None, :]) & (position[:, None] != position[None, :])
    scores = jnp.where(allowed, scores, NEG_FILL)
    row_max = jnp.max(scores, axis=1, keepdims=True)
    raised = jnp.exp(scores - row_max)
    weights = raised / jnp.sum(raised, axis=1, keepdims=True)
    attended = jnp.einsum(
        "rc,cd->rd", weights.astype(jnp.bfloat16), tokens_v, preferred_element_type=jnp.float32
    )
    return (weights, attended)


def unit_backward(tokens_x, tokens_v, grad_rows, weights, attended):
    inv_root = tokens_x.shape[1] ** (-0.5)
    grad_weights = jnp.einsum("rd,cd->rc", grad_rows, tokens_v, preferred_element_type=jnp.float32)
    row_delta = jnp.sum(grad_rows.astype(jnp.float32) * attended, axis=1, keepdims=True)
    grad_scores = weights * (grad_weights - row_delta)
    symmetric = (grad_scores + grad_scores.T).astype(jnp.bfloat16)
    grad_x = (
        jnp.einsum("rc,cd->rd", symmetric, tokens_x, preferred_element_type=jnp.float32) * inv_root
    ).astype(jnp.bfloat16)
    grad_v = jnp.einsum(
        "rc,rd->cd", weights.astype(jnp.bfloat16), grad_rows, preferred_element_type=jnp.float32
    ).astype(jnp.bfloat16)
    return (grad_x, grad_v)


def forward_unit(operands):
    tokens_x, tokens_v, group = operands
    return unit_forward(tokens_x, tokens_v, group)


def backward_unit(operands):
    tokens_x, tokens_v, grad_rows, weights, attended = operands
    return unit_backward(tokens_x, tokens_v, grad_rows, weights, attended)


def to_slots(local, packing, seq_count):
    blocks_here = packing.shape[1]
    heads_here = packing.shape[2]
    head_width = local.shape[1] // heads_here
    shaped = local.reshape(blocks_here, BLOCK, heads_here, head_width)
    packed = jnp.einsum(
        "ptk,trkd->prd", packing, shaped, preferred_element_type=jnp.float32
    ).astype(jnp.bfloat16)
    return packed.reshape(seq_count, -1, head_width)


def from_slots(arrived, packing):
    head_width = arrived.shape[-1]
    flat = arrived.reshape(packing.shape[0], BLOCK, head_width)
    placed = jnp.einsum("ptk,prd->trkd", packing, flat, preferred_element_type=jnp.float32).astype(
        jnp.bfloat16
    )
    return placed.reshape(packing.shape[1] * BLOCK, packing.shape[2] * head_width)


def to_units(arrived, picking, unit_count):
    head_width = arrived.shape[-1]
    flat = arrived.reshape(picking.shape[1], BLOCK, head_width)
    gathered = jnp.einsum("up,prd->urd", picking, flat, preferred_element_type=jnp.float32).astype(
        jnp.bfloat16
    )
    return gathered.reshape(unit_count, -1, head_width)


def from_units(results, picking, seq_count):
    head_width = results.shape[-1]
    flat = results.reshape(picking.shape[0], BLOCK, head_width)
    placed = jnp.einsum("up,urd->prd", picking, flat, preferred_element_type=jnp.float32).astype(
        jnp.bfloat16
    )
    return placed.reshape(seq_count, -1, head_width)


def model_output(attended, out_weight):
    partial_term = jnp.dot(attended, out_weight, preferred_element_type=jnp.float32)
    return lax.psum_scatter(
        partial_term.astype(jnp.bfloat16), "head", scatter_dimension=1, tiled=True
    )


def cotangent_heads(out_cotangent, out_weight):
    summed = jnp.einsum(
        "tn,kn->tk",
        lax.all_gather(out_cotangent, "head", axis=1, tiled=True),
        out_weight,
        preferred_element_type=jnp.float32,
    )
    return summed.astype(jnp.bfloat16)


def per_device(qk, values, out_weight, out_cotangent, cluster_ids):
    seq_count = lax.axis_size("seq")
    my_seq = lax.axis_index("seq")
    block_count = cluster_ids.shape[0]
    heads_here = cluster_ids.shape[1]
    blocks_here = qk.shape[0] // BLOCK
    item_count = blocks_here * heads_here
    per_peer = max(2, (item_count + seq_count - 1) // seq_count)
    slot_total = seq_count * per_peer
    owners = cluster_ids // CL_OWN
    item_owner = owners.reshape(seq_count, item_count)
    item_order = jnp.arange(item_count)
    before = item_order[None, :] < item_order[:, None]
    same_owner = item_owner[:, :, None] == item_owner[:, None, :]
    rank_sent = jnp.sum((same_owner & before[None, :, :]).astype(jnp.int32), axis=2)
    slot_index = item_owner * per_peer + rank_sent
    my_slots = lax.dynamic_index_in_dim(slot_index, my_seq, 0, keepdims=False)
    slot_range = jnp.arange(slot_total, dtype=jnp.int32)
    packing = (
        (slot_range[:, None] == my_slots[None, :])
        .astype(jnp.bfloat16)
        .reshape(slot_total, blocks_here, heads_here)
    )
    source_seq = jnp.arange(seq_count, dtype=jnp.int32)[:, None]
    arrival_slot = source_seq * per_peer + rank_sent
    received = (owners == my_seq).T.astype(jnp.int32)
    source_slot = arrival_slot.reshape(block_count, heads_here).T
    position = jnp.cumsum(received, axis=1) - received
    places = jnp.arange(blocks_here, dtype=jnp.int32)
    chosen = (received[:, None, :] == 1) & (position[:, None, :] == places[None, :, None])
    unit_slot = jnp.sum(jnp.where(chosen, source_slot[:, None, :], 0), axis=2)
    unit_group = jnp.sum(jnp.where(chosen, cluster_ids.T[:, None, :], 0), axis=2)
    picking = (unit_slot.reshape(-1)[:, None] == slot_range[None, :]).astype(jnp.bfloat16)
    send_x = to_slots(qk, packing, seq_count)
    send_v = to_slots(values, packing, seq_count)
    arrived_x, arrived_v = (
        lax.all_to_all(send_x, "seq", split_axis=0, concat_axis=0, tiled=True),
        lax.all_to_all(send_v, "seq", split_axis=0, concat_axis=0, tiled=True),
    )
    unit_x = to_units(arrived_x, picking, heads_here)
    unit_v = to_units(arrived_v, picking, heads_here)
    weights, unit_att = lax.map(forward_unit, (unit_x, unit_v, unit_group))
    home_att = lax.all_to_all(
        from_units(unit_att.astype(jnp.bfloat16), picking, seq_count),
        "seq",
        split_axis=0,
        concat_axis=0,
        tiled=True,
    )
    attended = from_slots(home_att, packing)
    output = model_output(attended, out_weight)
    grad_attended = cotangent_heads(out_cotangent, out_weight)
    arrived_g = lax.all_to_all(
        to_slots(grad_attended, packing, seq_count), "seq", split_axis=0, concat_axis=0, tiled=True
    )
    unit_g = to_units(arrived_g, picking, heads_here)
    unit_gx, unit_gv = lax.map(backward_unit, (unit_x, unit_v, unit_g, weights, unit_att))
    home_gx, home_gv = (
        lax.all_to_all(
            from_units(unit_gx, picking, seq_count), "seq", split_axis=0, concat_axis=0, tiled=True
        ),
        lax.all_to_all(
            from_units(unit_gv, picking, seq_count), "seq", split_axis=0, concat_axis=0, tiled=True
        ),
    )
    grad_qk = from_slots(home_gx, packing)
    grad_values = from_slots(home_gv, packing)
    return (output, grad_qk, grad_values)


def solution(mesh):
    return jax.shard_map(
        per_device,
        mesh=mesh,
        in_specs=(
            P("seq", "head"),
            P("seq", "head"),
            P("head", None),
            P("seq", "head"),
            P(None, "head"),
        ),
        out_specs=(P("seq", "head"), P("seq", "head"), P("seq", "head")),
        check_vma=False,
    )
```

profile of v0, /device:TPU:16, one launch (start us, length us, event | category | flops | bytes accessed | tf_op | source)
XLA Modules:
  0.0 683.7 jit_solution(4577155340845065639)
XLA Ops:
  11.8 4.6 copy.60
  16.4 12.2 %all-to-all-start = ((bf16[64,256,128]{2,1,0:T(8,128)(2,1)}), bf16[64,256,128]{2,1,0:T(8,128)(2,1)}, u32[]{:S(2)}, u32[]{:S(2)}) async-start(bf16[64,256,128]{2,1,0:T(8,128)(2,1)} %bitcast.193), calls=%async_computation | async-start | bytes 8388608 | tf_op jit(solution)/shard_map/all_to_all | solution.py:147
  31.4 4.7 copy.64
  36.0 88.8 %all-to-all-done = bf16[64,256,128]{2,1,0:T(8,128)(2,1)} async-done(((bf16[64,256,128]{2,1,0:T(8,128)(2,1)}), bf16[64,256,128]{2,1,0:T(8,128)(2,1)}, u32[]{:S(2)}, u32[]{:S(2)}) %all-to-all-start) | async-done | bytes 4194336 | tf_op jit(solution)/shard_map/all_to_all | solution.py:147
  124.8 5.8 all-to-all-start.1
  134.1 50.2 %all-gather.2.cloned.1.call-done = bf16[1024,2048]{1,0:T(8,128)(2,1)} async-done(((bf16[1024,512]{1,0:T(8,128)(2,1)}), bf16[1024,2048]{1,0:T(8,128)(2,1)}) %all-gather.2.cloned.1.call-update) | async-done | bytes 4194320 | tf_op jit(solution)/shard_map/all_gather | solution.py:104
  184.3 5.5 convolution_convert_fusion.4
  192.6 4.6 copy.73
  197.2 4.8 fusion.70
  202.4 24.5 %all-to-all-done.1 = bf16[64,256,128]{2,1,0:T(8,128)(2,1)} async-done(((bf16[64,256,128]{2,1,0:T(8,128)(2,1)}), bf16[64,256,128]{2,1,0:T(8,128)(2,1)}, u32[]{:S(2)}, u32[]{:S(2)}) %all-to-all-start.1) | async-done | bytes 4194336 | tf_op jit(solution)/shard_map/all_to_all | solution.py:148
  226.9 6.1 all-to-all-start.3
  233.0 4.8 fusion.73
  239.2 27.8 %while.24 = (s32[]{:T(128)}, f32[4,1024,1024]{1,2,0:T(8,128)}, f32[4,1024,128]{2,1,0:T(8,128)}, s32[4,8]{1,0:T(4,128)S(1)}, bf16[4,1024,128]{2,1,0:T(8,128)(2,1)S(1)}, /*index=5*/bf16[4,1024,128]{2,1,0:T(8,128)(2,1)}, s32[]{:T(128)}) while((s32[]{:T(128)}, f32[4,1024,1024]{1,2,0:T(8,128)}, f32[4,1024,128]{2,1,0:T(8,128)}, ...), condition=%wide.region_8.9_spmd, body=%wide.region_5.8_spmd.sunk | while | flops 550500352 | bytes 22062772 | solution.py:152
  241.0 2.5 bitcast_dynamic-update-slice_fusion.2
  243.5 2.6 fusion.160
  247.9 2.5 bitcast_dynamic-update-slice_fusion.2
  250.5 2.6 fusion.160
  254.9 2.5 bitcast_dynamic-update-slice_fusion.2
  257.4 2.6 fusion.160
  261.8 2.5 bitcast_dynamic-update-slice_fusion.2
  264.4 2.6 fusion.160
  266.9 2.1 convert_element_type.93
  270.4 4.7 copy.68
  275.1 54.1 %all-to-all-done.3 = bf16[64,256,128]{2,1,0:T(8,128)(2,1)} async-done(((bf16[64,256,128]{2,1,0:T(8,128)(2,1)}), bf16[64,256,128]{2,1,0:T(8,128)(2,1)}, u32[]{:S(2)}, u32[]{:S(2)}) %all-to-all-start.3) | async-done | bytes 4194336 | tf_op jit(solution)/shard_map/all_to_all | solution.py:163
  329.2 5.8 all-to-all-start.2
  335.0 4.8 fusion.76
  340.3 112.8 %while.25 = (s32[]{:T(128)}, bf16[4,1024,128]{2,1,0:T(8,128)(2,1)}, bf16[4,1024,128]{2,1,0:T(8,128)(2,1)}, f32[4,1024,1024]{1,2,0:T(8,128)}, bf16[4,1024,128]{2,...) while((s32[]{:T(128)}, bf16[4,1024,128]{2,1,0:T(8,128)(2,1)}, ...), condition=%wide.region_12.13_spmd, body=%wide.region_10.12_spmd.sunk | while | flops 811334656 | bytes 65285248 | solution.py:167
  341.5 4.7 constant_dynamic-slice_fusion.3
  346.3 5.3 copy.159
  351.6 4.9 bitcast_multiply_fusion.3
  356.5 5.4 copy.160
  361.9 5.1 fusion.168
  367.0 1.5 fusion.169
  369.7 4.7 constant_dynamic-slice_fusion.3
  374.5 5.3 copy.159
  379.8 4.9 bitcast_multiply_fusion.3
  384.7 5.4 copy.160
  390.1 5.1 fusion.168
  395.2 1.5 fusion.169
  397.9 4.7 constant_dynamic-slice_fusion.3
  402.7 5.3 copy.159
  408.0 4.9 bitcast_multiply_fusion.3
  412.9 5.4 copy.160
  418.3 5.1 fusion.168
  423.4 1.5 fusion.169
  426.1 4.7 constant_dynamic-slice_fusion.3
  430.9 5.3 copy.159
  436.2 4.9 bitcast_multiply_fusion.3
  441.1 5.4 copy.160
  446.5 5.1 fusion.168
  453.1 2.6 convolution_convert_fusion.2
  455.7 4.7 copy.78
  460.4 10.9 %all-to-all-start.4 = ((bf16[64,256,128]{2,1,0:T(8,128)(2,1)}), bf16[64,256,128]{2,1,0:T(8,128)(2,1)}, u32[]{:S(2)}, u32[]{:S(2)}) async-start(bf16[64,256,128]{2,1,0:T(8,128)(2,1)} %bitcast.192), calls=%async_computation.5 | async-start | bytes 8388608 | tf_op jit(solution)/shard_map/all_to_all | solution.py:169
  471.2 2.6 convolution_convert_fusion.1
  473.8 4.7 copy.82
  478.5 88.9 %all-to-all-done.4 = bf16[64,256,128]{2,1,0:T(8,128)(2,1)} async-done(((bf16[64,256,128]{2,1,0:T(8,128)(2,1)}), bf16[64,256,128]{2,1,0:T(8,128)(2,1)}, u32[]{:S(2)}, u32[]{:S(2)}) %all-to-all-start.4) | async-done | bytes 4194336 | tf_op jit(solution)/shard_map/all_to_all | solution.py:169
  567.5 5.8 all-to-all-start.5
  573.3 4.8 fusion.94
  578.1 2.0 copy.71
  580.1 5.6 convolution_convert_fusion
  585.7 4.8 fusion.91
  591.0 78.5 %all-to-all-done.5 = bf16[64,256,128]{2,1,0:T(8,128)(2,1)} async-done(((bf16[64,256,128]{2,1,0:T(8,128)(2,1)}), bf16[64,256,128]{2,1,0:T(8,128)(2,1)}, u32[]{:S(2)}, u32[]{:S(2)}) %all-to-all-start.5) | async-done | bytes 4194336 | tf_op jit(solution)/shard_map/all_to_all | solution.py:172
  669.5 4.8 fusion.88
  674.7 1.7 copy_bitcast_fusion
  (85 shorter events, 31.7 us)
Async XLA Ops:
  7.2 177.1 %copy-start = (bf16[512,2048]{1,0:T(8,128)(2,1)S(1)}, bf16[512,2048]{1,0:T(8,128)(2,1)}, u32[]{:S(2)}) copy-start(bf16[512,2048]{1,0:T(8,128)(2,1)} %param.11) | copy-start | bytes 6291460
  9.0 182.1 %copy-start.3 = (s32[8,4]{0,1:T(4,128)}, s32[8,4]{0,1:T(4,128)S(1)}, u32[]{:S(2)}) copy-start(s32[8,4]{0,1:T(4,128)S(1)} %copy.58) | copy-start | bytes 388
  16.4 108.4 %all-to-all-start = ((bf16[64,256,128]{2,1,0:T(8,128)(2,1)}), bf16[64,256,128]{2,1,0:T(8,128)(2,1)}, u32[]{:S(2)}, u32[]{:S(2)}) async-start(bf16[64,256,128]{2,1,0:T(8,128)(2,1)} %bitcast.193), calls=%async_computation | async-start | bytes 8388608 | tf_op jit(solution)/shard_map/all_to_all | solution.py:147
  124.8 8.9 %copy-start.5 = (s32[512,4]{0,1:T(4,128)S(1)}, s32[512,4]{0,1:T(4,128)}, u32[]{:S(2)}) copy-start(s32[512,4]{0,1:T(4,128)} %param.13) | copy-start | bytes 24580
  124.8 102.0 %all-to-all-start.1 = ((bf16[64,256,128]{2,1,0:T(8,128)(2,1)}), bf16[64,256,128]{2,1,0:T(8,128)(2,1)}, u32[]{:S(2)}, u32[]{:S(2)}) async-start(bf16[64,256,128]{2,1,0:T(8,128)(2,1)} %bitcast.190), calls=%async_computation.1 | async-start | bytes 8388608 | tf_op jit(solution)/shard_map/all_to_all | solution.py:148
  130.6 53.7 %all-gather.2.cloned.1.call-start = ((), (), s32[]{:S(2)}) async-start(), calls=%async_computation.8 | async-start | bytes 5242880 | tf_op jit(solution)/shard_map/all_gather | solution.py:104
  226.9 102.3 %all-to-all-start.3 = ((bf16[64,256,128]{2,1,0:T(8,128)(2,1)}), bf16[64,256,128]{2,1,0:T(8,128)(2,1)}, u32[]{:S(2)}, u32[]{:S(2)}) async-start(bf16[64,256,128]{2,1,0:T(8,128)(2,1)} %bitcast.188), calls=%async_computation.4 | async-start | bytes 8388608 | tf_op jit(solution)/shard_map/all_to_all | solution.py:163
  266.9 3.5 copy-start.2
  329.2 131.2 %all-to-all-start.2 = ((bf16[64,256,128]{2,1,0:T(8,128)(2,1)}), bf16[64,256,128]{2,1,0:T(8,128)(2,1)}, u32[]{:S(2)}, u32[]{:S(2)}) async-start(bf16[64,256,128]{2,1,0:T(8,128)(2,1)} %bitcast.189), calls=%async_computation.2 | async-start | bytes 8388608 | tf_op jit(solution)/shard_map/all_to_all | solution.py:153
  361.9 5.1 copy-start.1
  390.1 5.1 copy-start.1
  418.3 5.1 copy-start.1
  446.5 5.1 copy-start.1
  460.4 107.1 %all-to-all-start.4 = ((bf16[64,256,128]{2,1,0:T(8,128)(2,1)}), bf16[64,256,128]{2,1,0:T(8,128)(2,1)}, u32[]{:S(2)}, u32[]{:S(2)}) async-start(bf16[64,256,128]{2,1,0:T(8,128)(2,1)} %bitcast.192), calls=%async_computation.5 | async-start | bytes 8388608 | tf_op jit(solution)/shard_map/all_to_all | solution.py:169
  567.4 5.9 copy-start.4
  567.5 102.0 %all-to-all-start.5 = ((bf16[64,256,128]{2,1,0:T(8,128)(2,1)}), bf16[64,256,128]{2,1,0:T(8,128)(2,1)}, u32[]{:S(2)}, u32[]{:S(2)}) async-start(bf16[64,256,128]{2,1,0:T(8,128)(2,1)} %bitcast.191), calls=%async_computation.6 | async-start | bytes 8388608 | tf_op jit(solution)/shard_map/all_to_all | solution.py:172
  573.3 103.2 %reduce-scatter.2.cloned.1.call-start = ((), (), s32[]{:S(2)}) async-start(), calls=%async_computation.7 | async-start | bytes 5242880 | tf_op jit(solution)/shard_map/reduce_scatter | solution.py:96
Sparse Core Ops, SparseCore 0:
  133.3 50.9 all-gather.1
  585.8 48.8 reduce-scatter.1
where the time goes:
time: 694 us; the launch traced here: 684 us
  waiting for transfers between devices  386 us (56%)
  matrix products  111 us (16%)
  local copies, waits for them, and re-layouts  102 us (15%)
  starting transfers between devices  46.9 us (7%)
  other arithmetic  22.8 us (3%)
  between operations  14.8 us (2%)
    all_to_all x1, waiting for transfers between devices, per_device(): lax.all_to_all(from_units(unit_gx, picking, seq_count), 'seq', split_axis...  88.9 us
    all_to_all x1, waiting for transfers between devices, per_device(): lax.all_to_all(send_x, 'seq', split_axis=0, concat_axis=0, tiled=True)  88.8 us
    all_to_all x1, waiting for transfers between devices, per_device(): lax.all_to_all(from_units(unit_gv, picking, seq_count), 'seq', split_axis...  78.5 us
    all_to_all x1, waiting for transfers between devices, per_device(): lax.all_to_all(to_slots(grad_attended, packing, seq_count), 'seq', split_...  54.1 us
    all_gather x1, waiting for transfers between devices, cotangent_heads(): lax.all_gather(out_cotangent, 'head', axis=1, tiled=True)  50.2 us
    dynamic_slice x8, local copies, waits for them, and re-layouts, per_device(): lax.map(backward_unit, (unit_x, unit_v, unit_g, weights, unit_att))  40.2 us
    all_to_all x1, waiting for transfers between devices, per_device(): lax.all_to_all(send_v, 'seq', split_axis=0, concat_axis=0, tiled=True)  24.5 us
    mul x4, local copies, waits for them, and re-layouts, unit_backward(): grad_scores = weights * (grad_weights - row_delta)  21.5 us
  transfers between devices with their start and end apart: 8, of which 6 were waited for; matrix products, arithmetic and copies ran while one was open for 33% of the time, Pallas kernels for 0%

commit v1 on v0

--- a/solution.py
+++ b/solution.py
@@ -6,6 +6,11 @@
 BLOCK = 128
 CL_OWN = 2
 NEG_FILL = -1e30
+
+
+def swapped_in(block, mesh_axis, dim):
+    sent = jnp.stack([block] * lax.axis_size(mesh_axis))
+    return jnp.concatenate(lax.all_to_all(sent, mesh_axis, 0, 0), axis=dim)
 
 
 def unit_forward(tokens_x, tokens_v, group):
@@ -101,7 +106,7 @@
 def cotangent_heads(out_cotangent, out_weight):
     summed = jnp.einsum(
         "tn,kn->tk",
-        lax.all_gather(out_cotangent, "head", axis=1, tiled=True),
+        swapped_in(out_cotangent, "head", 1),
         out_weight,
         preferred_element_type=jnp.float32,
     )

time: 694 us -> 743 us (1.071)
  waiting for transfers between devices: 386 us -> 422 us
    all_to_all x1, waiting for transfers between devices: 24.5 us -> 75.4 us  [per_device(): lax.all_to_all(send_v, 'seq', split_axis=0, concat_axis=0, tiled=True)]
    all_gather x1 -> x0, waiting for transfers between devices: 50.2 us -> none  [cotangent_heads(): lax.all_gather(out_cotangent, 'head', axis=1, tiled=True)]
    all_to_all x0 -> x1, waiting for transfers between devices: none -> 35.9 us  [swapped_in(): return jnp.concatenate(lax.all_to_all(sent, mesh_axis, 0, 0), axis=dim)]
  transfers between devices with their start and end apart: 8 -> 8, of which waited for: 6 -> 6; matrix products, arithmetic and copies ran while one was open for 33% -> 32% of each run, Pallas kernels for 0% -> 0%
where the time goes in v1:
time: 743 us; the launch traced here: 730 us
  waiting for transfers between devices  422 us (57%)
  matrix products  112 us (15%)
  local copies, waits for them, and re-layouts  106 us (14%)
  starting transfers between devices  53.9 us (7%)
  other arithmetic  22 us (3%)
  between operations  14.7 us (2%)
    all_to_all x1, waiting for transfers between devices, per_device(): lax.all_to_all(from_units(unit_gx, picking, seq_count), 'seq', split_axis...  88.9 us
    all_to_all x1, waiting for transfers between devices, per_device(): lax.all_to_all(send_x, 'seq', split_axis=0, concat_axis=0, tiled=True)  88.8 us
    all_to_all x1, waiting for transfers between devices, per_device(): lax.all_to_all(from_units(unit_gv, picking, seq_count), 'seq', split_axis...  78.5 us
    all_to_all x1, waiting for transfers between devices, per_device(): lax.all_to_all(send_v, 'seq', split_axis=0, concat_axis=0, tiled=True)  75.4 us
    all_to_all x1, waiting for transfers between devices, per_device(): lax.all_to_all(to_slots(grad_attended, packing, seq_count), 'seq', split_...  54.1 us
    dynamic_slice x8, local copies, waits for them, and re-layouts, per_device(): lax.map(backward_unit, (unit_x, unit_v, unit_g, weights, unit_att))  40.2 us
    all_to_all x1, waiting for transfers between devices, swapped_in(): return jnp.concatenate(lax.all_to_all(sent, mesh_axis, 0, 0), axis=dim)  35.9 us
    mul x4, local copies, waits for them, and re-layouts, unit_backward(): grad_scores = weights * (grad_weights - row_delta)  21.5 us
  transfers between devices with their start and end apart: 8, of which 6 were waited for; matrix products, arithmetic and copies ran while one was open for 32% of the time, Pallas kernels for 0%

profile of v1, /device:TPU:16, one launch (start us, length us, event | category | flops | bytes accessed | tf_op | source)
XLA Modules:
  0.0 730.2 jit_solution(8987655272056433887)
XLA Ops:
  7.2 1.6 copy.73
  8.8 2.5 stack.2
  11.3 7.0 all-to-all-start.3
  22.1 4.7 copy.61
  26.7 35.9 %all-to-all-done.3 = bf16[4,1024,512]{1,2,0:T(8,128)(2,1)} async-done(((bf16[4,1024,512]{1,2,0:T(8,128)(2,1)}), bf16[4,1024,512]{1,2,0:T(8,128)(2,1)}, u32[]{:S(2)}, u32[]{:S(2)}) %all-to-all-start.3) | async-done | bytes 4194336 | tf_op jit(solution)/shard_map/all_to_all | solution.py:13
  62.7 12.3 %all-to-all-start = ((bf16[64,256,128]{2,1,0:T(8,128)(2,1)}), bf16[64,256,128]{2,1,0:T(8,128)(2,1)}, u32[]{:S(2)}, u32[]{:S(2)}) async-start(bf16[64,256,128]{2,1,0:T(8,128)(2,1)} %bitcast.196), calls=%async_computation | async-start | bytes 8388608 | tf_op jit(solution)/shard_map/all_to_all | solution.py:152
  77.8 4.7 copy.65
  82.4 88.8 %all-to-all-done = bf16[64,256,128]{2,1,0:T(8,128)(2,1)} async-done(((bf16[64,256,128]{2,1,0:T(8,128)(2,1)}), bf16[64,256,128]{2,1,0:T(8,128)(2,1)}, u32[]{:S(2)}, u32[]{:S(2)}) %all-to-all-start) | async-done | bytes 4194336 | tf_op jit(solution)/shard_map/all_to_all | solution.py:152
  171.2 5.9 all-to-all-start.1
  179.8 5.5 convolution_convert_fusion.4
  188.1 4.6 copy.75
  192.7 4.8 fusion.70
  198.0 75.4 %all-to-all-done.1 = bf16[64,256,128]{2,1,0:T(8,128)(2,1)} async-done(((bf16[64,256,128]{2,1,0:T(8,128)(2,1)}), bf16[64,256,128]{2,1,0:T(8,128)(2,1)}, u32[]{:S(2)}, u32[]{:S(2)}) %all-to-all-start.1) | async-done | bytes 4194336 | tf_op jit(solution)/shard_map/all_to_all | solution.py:153
  273.3 6.1 all-to-all-start.4
  279.4 4.8 fusion.73
  285.6 27.8 %while.24 = (s32[]{:T(128)}, f32[4,1024,1024]{1,2,0:T(8,128)}, f32[4,1024,128]{2,1,0:T(8,128)}, s32[4,8]{1,0:T(4,128)S(1)}, bf16[4,1024,128]{2,1,0:T(8,128)(2,1)S(1)}, /*index=5*/bf16[4,1024,128]{2,1,0:T(8,128)(2,1)}, s32[]{:T(128)}) while((s32[]{:T(128)}, f32[4,1024,1024]{1,2,0:T(8,128)}, f32[4,1024,128]{2,1,0:T(8,128)}, ...), condition=%wide.region_8.9_spmd, body=%wide.region_5.8_spmd.sunk | while | flops 550500352 | bytes 22062772 | solution.py:157
  287.5 2.5 bitcast_dynamic-update-slice_fusion.2
  290.0 2.6 fusion.160
  294.4 2.5 bitcast_dynamic-update-slice_fusion.2
  296.9 2.6 fusion.160
  301.4 2.5 bitcast_dynamic-update-slice_fusion.2
  303.9 2.6 fusion.160
  308.3 2.5 bitcast_dynamic-update-slice_fusion.2
  310.8 2.6 fusion.160
  313.4 2.1 convert_element_type.93
  316.9 4.7 copy.69
  321.6 54.1 %all-to-all-done.4 = bf16[64,256,128]{2,1,0:T(8,128)(2,1)} async-done(((bf16[64,256,128]{2,1,0:T(8,128)(2,1)}), bf16[64,256,128]{2,1,0:T(8,128)(2,1)}, u32[]{:S(2)}, u32[]{:S(2)}) %all-to-all-start.4) | async-done | bytes 4194336 | tf_op jit(solution)/shard_map/all_to_all | solution.py:168
  375.7 5.8 all-to-all-start.2
  381.5 4.8 fusion.76
  386.7 112.8 %while.25 = (s32[]{:T(128)}, bf16[4,1024,128]{2,1,0:T(8,128)(2,1)}, bf16[4,1024,128]{2,1,0:T(8,128)(2,1)}, f32[4,1024,1024]{1,2,0:T(8,128)}, bf16[4,1024,128]{2,...) while((s32[]{:T(128)}, bf16[4,1024,128]{2,1,0:T(8,128)(2,1)}, ...), condition=%wide.region_12.13_spmd, body=%wide.region_10.12_spmd.sunk | while | flops 811334656 | bytes 65285248 | solution.py:172
  388.0 4.7 constant_dynamic-slice_fusion.3
  392.7 5.3 copy.161
  398.1 4.9 bitcast_multiply_fusion.3
  403.0 5.4 copy.162
  408.4 5.1 fusion.168
  416.2 4.7 constant_dynamic-slice_fusion.3
  421.0 5.3 copy.161
  426.3 4.9 bitcast_multiply_fusion.3
  431.2 5.4 copy.162
  436.6 5.1 fusion.168
  444.4 4.7 constant_dynamic-slice_fusion.3
  449.2 5.3 copy.161
  454.5 4.9 bitcast_multiply_fusion.3
  459.4 5.4 copy.162
  464.8 5.1 fusion.168
  472.6 4.7 constant_dynamic-slice_fusion.3
  477.4 5.3 copy.161
  482.7 4.9 bitcast_multiply_fusion.3
  487.6 5.4 copy.162
  493.0 5.1 fusion.168
  499.6 2.6 convolution_convert_fusion.2
  502.2 4.7 copy.80
  506.9 10.9 %all-to-all-start.5 = ((bf16[64,256,128]{2,1,0:T(8,128)(2,1)}), bf16[64,256,128]{2,1,0:T(8,128)(2,1)}, u32[]{:S(2)}, u32[]{:S(2)}) async-start(bf16[64,256,128]{2,1,0:T(8,128)(2,1)} %bitcast.195), calls=%async_computation.6 | async-start | bytes 8388608 | tf_op jit(solution)/shard_map/all_to_all | solution.py:174
  517.8 2.6 convolution_convert_fusion.1
  520.4 4.7 copy.84
  525.0 88.9 %all-to-all-done.5 = bf16[64,256,128]{2,1,0:T(8,128)(2,1)} async-done(((bf16[64,256,128]{2,1,0:T(8,128)(2,1)}), bf16[64,256,128]{2,1,0:T(8,128)(2,1)}, u32[]{:S(2)}, u32[]{:S(2)}) %all-to-all-start.5) | async-done | bytes 4194336 | tf_op jit(solution)/shard_map/all_to_all | solution.py:174
  614.0 5.8 all-to-all-start.6
  619.8 4.8 fusion.94
  624.7 2.0 copy.72
  626.6 5.6 convolution_convert_fusion
  632.2 4.8 fusion.91
  637.5 78.5 %all-to-all-done.6 = bf16[64,256,128]{2,1,0:T(8,128)(2,1)} async-done(((bf16[64,256,128]{2,1,0:T(8,128)(2,1)}), bf16[64,256,128]{2,1,0:T(8,128)(2,1)}, u32[]{:S(2)}, u32[]{:S(2)}) %all-to-all-start.6) | async-done | bytes 4194336 | tf_op jit(solution)/shard_map/all_to_all | solution.py:177
  716.0 4.8 fusion.88
  721.2 1.7 copy_bitcast_fusion
  (86 shorter events, 34.6 us)
Async XLA Ops:
  7.2 172.7 %copy-start = (bf16[512,2048]{1,0:T(8,128)(2,1)S(1)}, bf16[512,2048]{1,0:T(8,128)(2,1)}, u32[]{:S(2)}) copy-start(bf16[512,2048]{1,0:T(8,128)(2,1)} %param.11) | copy-start | bytes 6291460
  11.3 7.0 copy-start.5
  11.3 51.4 %all-to-all-start.3 = ((bf16[4,1024,512]{1,2,0:T(8,128)(2,1)}), bf16[4,1024,512]{1,2,0:T(8,128)(2,1)}, u32[]{:S(2)}, u32[]{:S(2)}) async-start(bf16[4,1024,512]{1,2,0:T(8,128)(2,1)} %stack.2), calls=%async_computation.4 | async-start | bytes 8388608 | tf_op jit(solution)/shard_map/all_to_all | solution.py:13
  19.3 167.4 %copy-start.3 = (s32[8,4]{0,1:T(4,128)}, s32[8,4]{0,1:T(4,128)S(1)}, u32[]{:S(2)}) copy-start(s32[8,4]{0,1:T(4,128)S(1)} %copy.59) | copy-start | bytes 388
  62.7 108.6 %all-to-all-start = ((bf16[64,256,128]{2,1,0:T(8,128)(2,1)}), bf16[64,256,128]{2,1,0:T(8,128)(2,1)}, u32[]{:S(2)}, u32[]{:S(2)}) async-start(bf16[64,256,128]{2,1,0:T(8,128)(2,1)} %bitcast.196), calls=%async_computation | async-start | bytes 8388608 | tf_op jit(solution)/shard_map/all_to_all | solution.py:152
  171.2 102.1 %all-to-all-start.1 = ((bf16[64,256,128]{2,1,0:T(8,128)(2,1)}), bf16[64,256,128]{2,1,0:T(8,128)(2,1)}, u32[]{:S(2)}, u32[]{:S(2)}) async-start(bf16[64,256,128]{2,1,0:T(8,128)(2,1)} %bitcast.193), calls=%async_computation.1 | async-start | bytes 8388608 | tf_op jit(solution)/shard_map/all_to_all | solution.py:153
  273.3 102.3 %all-to-all-start.4 = ((bf16[64,256,128]{2,1,0:T(8,128)(2,1)}), bf16[64,256,128]{2,1,0:T(8,128)(2,1)}, u32[]{:S(2)}, u32[]{:S(2)}) async-start(bf16[64,256,128]{2,1,0:T(8,128)(2,1)} %bitcast.191), calls=%async_computation.5 | async-start | bytes 8388608 | tf_op jit(solution)/shard_map/all_to_all | solution.py:168
  313.4 3.5 copy-start.2
  375.7 131.2 %all-to-all-start.2 = ((bf16[64,256,128]{2,1,0:T(8,128)(2,1)}), bf16[64,256,128]{2,1,0:T(8,128)(2,1)}, u32[]{:S(2)}, u32[]{:S(2)}) async-start(bf16[64,256,128]{2,1,0:T(8,128)(2,1)} %bitcast.192), calls=%async_computation.2 | async-start | bytes 8388608 | tf_op jit(solution)/shard_map/all_to_all | solution.py:158
  408.4 5.1 copy-start.1
  436.6 5.1 copy-start.1
  464.8 5.1 copy-start.1
  493.0 5.1 copy-start.1
  506.9 107.1 %all-to-all-start.5 = ((bf16[64,256,128]{2,1,0:T(8,128)(2,1)}), bf16[64,256,128]{2,1,0:T(8,128)(2,1)}, u32[]{:S(2)}, u32[]{:S(2)}) async-start(bf16[64,256,128]{2,1,0:T(8,128)(2,1)} %bitcast.195), calls=%async_computation.6 | async-start | bytes 8388608 | tf_op jit(solution)/shard_map/all_to_all | solution.py:174
  614.0 5.9 copy-start.4
  614.0 102.0 %all-to-all-start.6 = ((bf16[64,256,128]{2,1,0:T(8,128)(2,1)}), bf16[64,256,128]{2,1,0:T(8,128)(2,1)}, u32[]{:S(2)}, u32[]{:S(2)}) async-start(bf16[64,256,128]{2,1,0:T(8,128)(2,1)} %bitcast.194), calls=%async_computation.7 | async-start | bytes 8388608 | tf_op jit(solution)/shard_map/all_to_all | solution.py:177
  619.8 103.2 %reduce-scatter.2.cloned.1.call-start = ((), (), s32[]{:S(2)}) async-start(), calls=%async_computation.8 | async-start | bytes 5242880 | tf_op jit(solution)/shard_map/reduce_scatter | solution.py:101
Sparse Core Ops, SparseCore 0:
  632.4 49.4 reduce-scatter.1
